TPU v7x, 256 devices: a whole 4x4x8 slice. The times are simulated.
256 devices in a mesh: row: 16 (over z_lo, x, core), col: 16 (over z_hi, y).
Axes of the slice: x: 4, y: 4, z: 8 (z_hi: 4, z_lo: 2; z = z_hi * 2 + z_lo), core: 2. Of those that a mesh axis runs over, the one named last changes fastest.
Arguments:
- blocks_inverse: bfloat16 [12288, 12288], P('row', 'col'), as said below
- factor_rows: bfloat16 [2, 6144, 256], P(None, 'row'), may hold values from -0.15234375 to 0.15234375
- block_lists: int32 [2, 48], replicated, may hold values from 0 to 95, as said below
- diag_inverse: float32 [2, 256, 256], replicated, as said below
Outputs:
- column_inverse: float32 [2, 12288, 256], P(None, 'row')
- mirror_inverse: float32 [2, 256, 12288], P(None, None, 'col')
- diagonal_inverse: float32 [2, 256, 256], replicated
Inputs may be any that keep to these rules, and one draw needn't show every extreme that they name: blocks_inverse is exactly symmetric and positive definite. block_lists[s, m] is 2 * m or 2 * m + 1. diag_inverse[s] is symmetric.
All inputs are finite; a program needn't handle non-finite values.
Results may differ from a plain program's by a relative error of at most 0.0003.
Values may be sent and summed in bfloat16 or wider, within the bound.
A program may use at most 64 MiB of HBM per device.

v0:
```python
import jax
import jax.numpy as jnp
from jax import lax
from jax.sharding import PartitionSpec as P

BS = 128


def broadcast(x, axis, root):
    mine = lax.axis_index(axis) == root
    return lax.psum(jnp.where(mine, x, jnp.zeros_like(x)), axis)


def pair_bits(block_lists, first_block, block_count):
    local_lists = lax.dynamic_slice_in_dim(block_lists, first_block // 2, block_count // 2, 1)
    pair_first = 2 * (first_block // 2 + jnp.arange(block_count // 2, dtype=jnp.int32))
    return local_lists - pair_first[None, :]


def expand_pairs(packed, bits):
    sup_count = packed.shape[0]
    feature_count = packed.shape[2]
    pairs = bits.shape[1]
    grouped = packed.reshape(sup_count, pairs, 1, BS, feature_count)
    which = (
        bits[:, :, None, None, None] == jnp.arange(2, dtype=jnp.int32)[None, None, :, None, None]
    )
    dense = jnp.where(which, grouped, jnp.zeros((), packed.dtype))
    return dense.reshape(sup_count, pairs * 2 * BS, feature_count)


def compact_pairs(dense, bits):
    sup_count = dense.shape[0]
    feature_count = dense.shape[2]
    pairs = bits.shape[1]
    grouped = dense.reshape(sup_count, pairs, 2, BS, feature_count)
    chosen = jnp.where(bits[:, :, None, None] == 0, grouped[:, :, 0], grouped[:, :, 1])
    return chosen.reshape(sup_count, pairs * BS, feature_count)


def multiply_each(matrix, stacked):
    results = []
    for sup_index in range(stacked.shape[0]):
        results.append(
            jnp.dot(matrix, stacked[sup_index].astype(jnp.float32), precision=lax.Precision.HIGHEST)
        )
    return jnp.stack(results)


def local(blocks_inverse, factor_rows, block_lists, diag_inverse):
    row_index = lax.axis_index("row")
    col_index = lax.axis_index("col")
    row_blocks = blocks_inverse.shape[0] // BS
    col_blocks = blocks_inverse.shape[1] // BS
    row_bits = pair_bits(block_lists, row_index * row_blocks, row_blocks)
    col_bits = pair_bits(block_lists, col_index * col_blocks, col_blocks)
    packed_length = col_blocks // 2 * BS
    root_row = col_index * col_blocks // row_blocks
    gathered = lax.all_gather(factor_rows, "row", axis=1, tiled=True)
    column_packed = lax.dynamic_slice_in_dim(gathered, col_index * packed_length, packed_length, 1)
    column_dense = expand_pairs(column_packed, col_bits)
    blocks_wide = blocks_inverse.astype(jnp.float32)
    products = multiply_each(blocks_wide, column_dense)
    listed_products = compact_pairs(products, row_bits)
    diagonal_terms = jnp.einsum(
        "srw,srv->swv",
        factor_rows.astype(jnp.float32),
        listed_products,
        precision=lax.Precision.HIGHEST,
    )
    diagonal_inverse = diag_inverse + lax.psum(diagonal_terms, ("row", "col"))
    row_total = lax.psum(listed_products, "col")
    column_inverse = -expand_pairs(row_total, row_bits)
    mirror_total = broadcast(row_total, "row", root_row)
    mirror_inverse = jnp.transpose(-expand_pairs(mirror_total, col_bits), (0, 2, 1))
    return (column_inverse, mirror_inverse, diagonal_inverse)


def solution(mesh):
    return jax.shard_map(
        local,
        mesh=mesh,
        in_specs=(P("row", "col"), P(None, "row", None), P(), P()),
        out_specs=(P(None, "row", None), P(None, None, "col"), P()),
        check_vma=False,
    )
```

profile of v0, /device:TPU:1, one launch (start us, length us, event | category | flops | bytes accessed | tf_op | source)
XLA Modules:
  0.0 641.8 jit_solution(4474671392308871341)
XLA Ops:
  7.2 0.0 copy-start
  7.2 0.0 all-gather.2.cloned.1.call-start
  7.2 0.7 all-gather.2.cloned.1.call-update
  8.0 0.8 broadcast_compare_fusion
  8.7 0.1 broadcast_bitcast_fusion
  8.8 0.8 dynamic-slice_subtract_fusion
  9.6 0.1 iota_compare_fusion
  9.6 49.3 %all-gather.2.cloned.1.call-done = bf16[2,6144,256]{2,1,0:T(8,128)(2,1)} async-done(((bf16[2,384,256]{2,1,0:T(8,128)(2,1)}), bf16[2,6144,256]{2,1,0:T(8,128)(2,1)}) %all-gather.2.cloned.1.call-update) | async-done | bytes 6291472 | tf_op jit(solution)/shard_map/all_gather | solution.py:59
  59.0 1.0 constant_dynamic-slice_fusion
  60.0 0.1 broadcast_select_fusion
  60.1 0.8 fusion.1
  60.9 0.0 copy-done
  60.9 0.5 convolution_bitcast_fusion.1
  61.4 0.4 stack.9
  61.9 1.5 convolution_bitcast_fusion
  63.4 0.4 stack.10
  63.8 0.3 constant_dynamic-update-slice_fusion.1
  64.1 0.3 constant_dynamic-update-slice_fusion
  64.4 1.2 fusion
  65.6 1.0 copy.11
  66.6 1.0 copy.10
  67.6 0.2 broadcast_select_fusion.2
  67.8 0.0 copy-start.1
  67.8 3.0 convolution_bitcast_fusion.2
  70.8 0.0 all-reduce.4.cloned.1.call-start
  70.8 0.0 copy-done.1
  70.8 0.7 all-reduce.4.cloned.1.call-update
  71.5 0.0 copy-start.3
  71.5 0.0 all-reduce.8.cloned.1.call-start
  71.6 0.7 all-reduce.8.cloned.1.call-update
  72.2 0.0 all-reduce.6.cloned.1.call-start
  72.3 160.2 %all-reduce.4.cloned.1.call-done = f32[2,384,256]{2,1,0:T(8,128)} async-done(((f32[2,384,256]{2,1,0:T(8,128)}), f32[2,384,256]{2,1,0:T(8,128)}) %all-reduce.4.cloned.1.call-update) | async-done | bytes 786448 | tf_op jit(solution)/shard_map/psum | solution.py:72
  232.5 0.9 broadcast_select_fusion.1
  233.5 0.0 all-reduce.6.cloned.1.call-update
  233.5 0.1 iota_compare_fusion.1
  233.6 0.1 broadcast_in_dim.93
  233.7 0.1 broadcast_in_dim.107
  233.8 0.0 copy-done.3
  233.8 0.2 copy.15
  234.0 0.0 copy-start.2
  234.0 267.5 %all-reduce.8.cloned.1.call-done = f32[2,256,256]{1,2,0:T(8,128)} async-done(((f32[2,256,256]{1,2,0:T(8,128)}), f32[2,256,256]{1,2,0:T(8,128)}) %all-reduce.8.cloned.1.call-update) | async-done | bytes 524304 | tf_op jit(solution)/shard_map/psum | solution.py:71
  501.5 1.1 add.48
  502.6 1.0 copy.17
  503.6 0.0 copy-done.2
  503.6 0.4 copy.12
  504.0 1.7 broadcast_in_dim.104
  505.7 2.5 broadcast_in_dim.105
  508.2 1.3 select_negate_fusion
  509.5 3.0 copy.16
  512.5 115.7 %all-reduce.6.cloned.1.call-done = f32[2,3,128,256]{3,2,1,0:T(8,128)} async-done(((f32[2,3,128,256]{3,2,1,0:T(8,128)}), f32[2,3,128,256]{3,2,1,0:T(8,128)}) %all-reduce.6.cloned.1.call-update) | async-done | bytes 786448 | tf_op jit(solution)/shard_map/psum | solution.py:11
  628.2 1.5 copy.13
  629.8 1.7 broadcast_in_dim.112
  631.4 2.5 broadcast_in_dim.113
  634.0 1.3 negate_bitcast_fusion
  (5 shorter events, 0.1 us)
Async XLA Ops:
  7.2 53.8 %copy-start = (bf16[768,768]{1,0:T(8,128)(2,1)S(1)}, bf16[768,768]{1,0:T(8,128)(2,1)}, u32[]{:S(2)}) copy-start(bf16[768,768]{1,0:T(8,128)(2,1)} %param.4) | copy-start | bytes 3538948
  7.2 51.8 %all-gather.2.cloned.1.call-start = ((), (), s32[]{:S(2)}) async-start(), calls=%async_computation | async-start | bytes 6684672 | tf_op jit(solution)/shard_map/all_gather | solution.py:59
  67.8 3.0 copy-start.1
  70.8 161.8 %all-reduce.4.cloned.1.call-start = ((), (), s32[]{:S(2)}) async-start(), calls=%async_computation.1 | async-start | bytes 1572864 | tf_op jit(solution)/shard_map/psum | solution.py:72
  71.5 162.3 %copy-start.3 = (f32[2,256,256]{2,1,0:T(8,128)S(1)}, f32[2,256,256]{2,1,0:T(8,128)}, u32[]{:S(2)}) copy-start(f32[2,256,256]{2,1,0:T(8,128)} %param.7) | copy-start | bytes 1572868
  71.5 430.0 %all-reduce.8.cloned.1.call-start = ((), (), s32[]{:S(2)}) async-start(), calls=%async_computation.3 | async-start | bytes 1048576 | tf_op jit(solution)/shard_map/psum | solution.py:71
  72.2 556.0 %all-reduce.6.cloned.1.call-start = ((), (), s32[]{:S(2)}) async-start(), calls=%async_computation.2 | async-start | bytes 1572864 | tf_op jit(solution)/shard_map/psum | solution.py:11
  234.0 269.6 %copy-start.2 = (f32[2,384,256]{2,1,0:T(8,128)S(1)}, f32[2,384,256]{2,1,0:T(8,128)}, u32[]{:S(2)}) copy-start(f32[2,384,256]{2,1,0:T(8,128)} %all-reduce.4.cloned.1.call-done) | copy-start | bytes 2359300
Sparse Core Ops, SparseCore 0:
  9.8 49.1 all-gather.1
  74.8 157.7 all-reduce.3
  238.6 262.8 all-reduce.7
  504.0 124.2 all-reduce.5
where the time goes:
time: 642 us
  waiting for transfers between devices  595 us (93%)
  local copies, waits for them, and re-layouts  21.3 us (3%)
  between operations  14 us (2%)
  other arithmetic  6.57 us (1%)
    psum x1, waiting for transfers between devices, local(): diagonal_inverse = diag_inverse + lax.psum(diagonal_terms, ('row', 'col'))  268 us
    psum x1, waiting for transfers between devices, local(): row_total = lax.psum(listed_products, 'col')  160 us
    psum x1, waiting for transfers between devices, broadcast(): return lax.psum(jnp.where(mine, x, jnp.zeros_like(x)), axis)  116 us
    all_gather x1, waiting for transfers between devices, local(): gathered = lax.all_gather(factor_rows, 'row', axis=1, tiled=True)  49.3 us
  transfers between devices with their start and end apart: 4, of which 4 were waited for; matrix products, arithmetic and copies ran while one was open for 2% of the time, Pallas kernels for 0%

commit v1 on v0

--- a/solution.py
+++ b/solution.py
@@ -8,7 +8,7 @@
 
 def broadcast(x, axis, root):
     mine = lax.axis_index(axis) == root
-    return lax.psum(jnp.where(mine, x, jnp.zeros_like(x)), axis)
+    return jnp.sum(lax.all_gather(jnp.where(mine, x, jnp.zeros_like(x)), axis), axis=0)
 
 
 def pair_bits(block_lists, first_block, block_count):

time: 642 us -> 597 us (0.930)
  waiting for transfers between devices: 595 us -> 545 us
    psum x1 -> x0, waiting for transfers between devices: 116 us -> none  [broadcast(): return lax.psum(jnp.where(mine, x, jnp.zeros_like(x)), axis)]
    all_gather x0 -> x1, waiting for transfers between devices: none -> 65.8 us  [broadcast(): lax.all_gather(jnp.where(mine, x, jnp.zeros_like(x)), axis)]
where the time goes in v1:
time: 597 us; the launch traced here: 596 us
  waiting for transfers between devices  545 us (91%)
  local copies, waits for them, and re-layouts  20.1 us (3%)
  between operations  14 us (2%)
  other arithmetic  12.1 us (2%)
    psum x1, waiting for transfers between devices, local(): diagonal_inverse = diag_inverse + lax.psum(diagonal_terms, ('row', 'col'))  268 us
    psum x1, waiting for transfers between devices, local(): row_total = lax.psum(listed_products, 'col')  160 us
    all_gather x1, waiting for transfers between devices, broadcast(): lax.all_gather(jnp.where(mine, x, jnp.zeros_like(x)), axis)  65.8 us
    all_gather x1, waiting for transfers between devices, local(): gathered = lax.all_gather(factor_rows, 'row', axis=1, tiled=True)  49.3 us
  transfers between devices with their start and end apart: 4, of which 4 were waited for; matrix products, arithmetic and copies ran while one was open for 2% of the time, Pallas kernels for 0%

profile of v1, /device:TPU:1, one launch (start us, length us, event | category | flops | bytes accessed | tf_op | source)
XLA Modules:
  0.0 596.3 jit_solution(1609241547857499951)
XLA Ops:
  7.2 0.0 copy-start
  7.2 0.0 all-gather.4.cloned.1.call-start
  7.2 0.7 all-gather.4.cloned.1.call-update
  8.0 0.8 broadcast_compare_fusion
  8.7 0.1 broadcast_bitcast_fusion
  8.8 0.8 dynamic-slice_subtract_fusion
  9.6 0.1 iota_compare_fusion
  9.6 49.3 %all-gather.4.cloned.1.call-done = bf16[2,6144,256]{2,1,0:T(8,128)(2,1)} async-done(((bf16[2,384,256]{2,1,0:T(8,128)(2,1)}), bf16[2,6144,256]{2,1,0:T(8,128)(2,1)}) %all-gather.4.cloned.1.call-update) | async-done | bytes 6291472 | tf_op jit(solution)/shard_map/all_gather | solution.py:59
  59.0 1.0 constant_dynamic-slice_fusion
  60.0 0.1 broadcast_select_fusion
  60.1 0.8 fusion.1
  60.9 0.0 copy-done
  60.9 0.5 convolution_bitcast_fusion.1
  61.4 0.4 stack.9
  61.9 1.5 convolution_bitcast_fusion
  63.4 0.4 stack.10
  63.8 0.3 constant_dynamic-update-slice_fusion.1
  64.1 0.3 constant_dynamic-update-slice_fusion
  64.4 1.2 fusion
  65.6 1.0 copy.19
  66.6 1.0 copy.18
  67.6 0.2 broadcast_select_fusion.2
  67.8 0.0 copy-start.1
  67.8 3.0 convolution_bitcast_fusion.2
  70.8 0.0 all-reduce.3.cloned.1.call-start
  70.8 0.0 copy-done.1
  70.8 0.7 all-reduce.3.cloned.1.call-update
  71.5 0.0 copy-start.3
  71.5 0.0 all-reduce.5.cloned.1.call-start
  71.6 0.7 all-reduce.5.cloned.1.call-update
  72.2 0.2 all-gather.6.cloned.1.call-start
  72.5 160.0 %all-reduce.3.cloned.1.call-done = f32[2,384,256]{2,1,0:T(8,128)} async-done(((f32[2,384,256]{2,1,0:T(8,128)}), f32[2,384,256]{2,1,0:T(8,128)}) %all-reduce.3.cloned.1.call-update) | async-done | bytes 786448 | tf_op jit(solution)/shard_map/psum | solution.py:72
  232.5 1.0 broadcast_select_fusion.1
  233.5 0.0 all-gather.6.cloned.1.call-update
  233.5 0.1 iota_compare_fusion.1
  233.6 0.1 broadcast_in_dim.93
  233.7 0.1 broadcast_in_dim.107
  233.8 0.0 copy-done.3
  233.8 0.2 copy.23
  234.0 0.0 copy-start.2
  234.0 267.5 %all-reduce.5.cloned.1.call-done = f32[2,256,256]{1,2,0:T(8,128)} async-done(((f32[2,256,256]{1,2,0:T(8,128)}), f32[2,256,256]{1,2,0:T(8,128)}) %all-reduce.5.cloned.1.call-update) | async-done | bytes 524304 | tf_op jit(solution)/shard_map/psum | solution.py:71
  501.5 1.1 add.46
  502.6 1.0 copy.25
  503.6 0.0 copy-done.2
  503.6 0.4 copy.20
  504.0 1.7 broadcast_in_dim.104
  505.7 2.5 broadcast_in_dim.105
  508.2 1.3 select_negate_fusion
  509.5 3.0 copy.24
  512.5 65.8 %all-gather.6.cloned.1.call-done = f32[32,384,256]{2,1,0:T(8,128)} async-done(((f32[2,384,256]{2,1,0:T(8,128)}), f32[32,384,256]{2,1,0:T(8,128)}) %all-gather.6.cloned.1.call-update) | async-done | bytes 12582928 | tf_op jit(solution)/shard_map/all_gather | solution.py:11
  578.3 5.5 reduce_sum.9
  583.8 0.4 copy.21
  584.2 1.7 broadcast_in_dim.112
  585.9 2.5 broadcast_in_dim.113
  588.4 1.3 negate_bitcast_fusion
  (5 shorter events, 0.1 us)
Async XLA Ops:
  7.2 53.8 %copy-start = (bf16[768,768]{1,0:T(8,128)(2,1)S(1)}, bf16[768,768]{1,0:T(8,128)(2,1)}, u32[]{:S(2)}) copy-start(bf16[768,768]{1,0:T(8,128)(2,1)} %param.4) | copy-start | bytes 3538948
  7.2 51.8 %all-gather.4.cloned.1.call-start = ((), (), s32[]{:S(2)}) async-start(), calls=%async_computation | async-start | bytes 6684672 | tf_op jit(solution)/shard_map/all_gather | solution.py:59
  67.8 3.0 copy-start.1
  70.8 161.7 %all-reduce.3.cloned.1.call-start = ((), (), s32[]{:S(2)}) async-start(), calls=%async_computation.1 | async-start | bytes 1572864 | tf_op jit(solution)/shard_map/psum | solution.py:72
  71.5 162.3 %copy-start.3 = (f32[2,256,256]{2,1,0:T(8,128)S(1)}, f32[2,256,256]{2,1,0:T(8,128)}, u32[]{:S(2)}) copy-start(f32[2,256,256]{2,1,0:T(8,128)} %param.7) | copy-start | bytes 1572868
  71.5 430.0 %all-reduce.5.cloned.1.call-start = ((), (), s32[]{:S(2)}) async-start(), calls=%async_computation.2 | async-start | bytes 1048576 | tf_op jit(solution)/shard_map/psum | solution.py:71
  72.2 506.1 %all-gather.6.cloned.1.call-start = ((), (), s32[]{:S(2)}) async-start(), calls=%async_computation.3 | async-start | bytes 13369344 | tf_op jit(solution)/shard_map/all_gather | solution.py:11
  234.0 269.6 %copy-start.2 = (f32[2,384,256]{2,1,0:T(8,128)S(1)}, f32[2,384,256]{2,1,0:T(8,128)}, u32[]{:S(2)}) copy-start(f32[2,384,256]{2,1,0:T(8,128)} %all-reduce.3.cloned.1.call-done) | copy-start | bytes 2359300
Sparse Core Ops, SparseCore 0:
  9.8 49.1 all-gather.3
  74.8 157.6 all-reduce.2
  238.5 262.8 all-reduce.4
  503.2 75.1 all-gather.5
